TPU v7x, 32 devices: a whole 2x2x4 slice. The times are simulated.
32 devices in a mesh: facet: 8 (over y, x, core), col: 4 (over z).
Axes of the slice: x: 2, y: 2, z: 4, core: 2. Of those that a mesh axis runs over, the one named last changes fastest.
Arguments:
- facets: float32 [2, 8, 24, 2, 4096], P(None, 'facet', None, None, 'col'), may hold values from -6 to 6
- facet_x: int32 [8], P('facet'), may hold values from 0 to 32767
- facet_y: int32 [2], replicated, may hold values from 0 to 32767
- col_u: int32 [8], replicated, may hold values from 0 to 32767
- slot_col: int32 [4, 8], P('col'), may hold values from 0 to 1
- slot_v: int32 [4, 8], P('col'), may hold values from 0 to 32767
Outputs:
- subgrids: float32 [4, 8, 512, 1024], P('col', 'facet')
Inputs may be any that keep to these rules, and one draw needn't show every extreme that they name: `col_u`: offset in the image. `slot_col`: the subgrid's column is owner * 2 + this value. `slot_v`: offset in the image.
All inputs are finite; a program needn't handle non-finite values.
Results may differ from a plain program's by a relative error of at most 0.0003.
Values sent between devices are 32-bit elements; how exact they have to be, the bound alone decides.
A program may use at most 128 MiB of HBM per device.

v0:
```python
import math
import jax
import jax.numpy as jnp
from jax import lax
from jax.sharding import PartitionSpec as P

FS = 4096
SG = 512
COLS_DEV = 2
SLOTS = 1


def mulmod(first_factor, second_factor, modulus):
    upper = first_factor * (second_factor // 512) % modulus
    return (upper * 512 + first_factor * (second_factor % 512)) % modulus


def column_part(real_part, imag_part, shifted, table, col_u, img, count):
    turn = 2.0 * math.pi / img
    column_angle = mulmod(col_u[:, None], shifted[None, :], img).astype(jnp.float32) * turn
    cosine = jnp.cos(column_angle)[:, None, :]
    sine = jnp.sin(column_angle)[:, None, :]
    turned_real = real_part[None] * cosine + imag_part[None] * sine
    turned_imag = imag_part[None] * cosine - real_part[None] * sine
    local_rows = real_part.shape[0]
    width = real_part.shape[1]
    stacked = jnp.stack([turned_real, turned_imag]).reshape(-1, width)
    product = jnp.dot(
        stacked, table, precision=lax.Precision.HIGHEST, preferred_element_type=jnp.float32
    )
    product = product.reshape(2, count, local_rows, 2 * SG)
    from_real = product[0]
    from_imag = product[1]
    real_out = from_real[..., :SG] + from_imag[..., SG:]
    imag_out = from_imag[..., :SG] - from_real[..., SG:]
    return jnp.concatenate([real_out, imag_out], axis=-1)


def slot_term(owned, row_cells, img, column, shift_v):
    turn = 2.0 * math.pi / img
    v_cells = (shift_v + jnp.arange(SG, dtype=jnp.int32)) % img
    angle = mulmod(v_cells[:, None], row_cells[None, :], img).astype(jnp.float32) * turn
    cosine = jnp.cos(angle)
    sine = jnp.sin(angle)
    chosen = lax.dynamic_index_in_dim(owned, column, 0, keepdims=False)
    first = jnp.dot(
        cosine, chosen, precision=lax.Precision.HIGHEST, preferred_element_type=jnp.float32
    )
    second = jnp.dot(
        sine, chosen, precision=lax.Precision.HIGHEST, preferred_element_type=jnp.float32
    )
    real_out = first[:, :SG] + second[:, SG:]
    imag_out = first[:, SG:] - second[:, :SG]
    return jnp.concatenate([real_out, imag_out], axis=-1)


def per_device(facets, facet_x, facet_y, col_u, slot_col, slot_v):
    width = facets.shape[-1]
    band_rows = facets.shape[2]
    img = FS * lax.axis_size("facet")
    turn = 2.0 * math.pi / img
    x_start = lax.axis_index("col") * width
    real_part = facets[:, 0, :, 0, :].reshape(-1, width)
    imag_part = facets[:, 0, :, 1, :].reshape(-1, width)
    shifted = (facet_x[0] + x_start + jnp.arange(width, dtype=jnp.int32)) % img
    u_cells = jnp.arange(SG, dtype=jnp.int32)
    table_angle = mulmod(u_cells[None, :], shifted[:, None], img).astype(jnp.float32) * turn
    table = jnp.concatenate([jnp.cos(table_angle), jnp.sin(table_angle)], axis=1)
    owned = lax.psum_scatter(
        column_part(
            real_part, imag_part, shifted, table, col_u, img, COLS_DEV * lax.axis_size("col")
        ),
        "col",
        scatter_dimension=0,
        tiled=True,
    )
    total_rows = owned.shape[1]
    row_ids = jnp.arange(total_rows, dtype=jnp.int32)
    y_start = jnp.where(row_ids // band_rows == 0, facet_y[0], facet_y[1])
    row_cells = (y_start + row_ids % band_rows) % img
    scale = 1.0 / math.sqrt(2.0 * FS * band_rows * lax.axis_size("facet"))
    owner_cols = slot_col[0]
    owner_shift = slot_v[0]
    merged = lax.psum(owned, "facet")

    def own_slot(slot_id):
        return slot_term(merged, row_cells, img, owner_cols[slot_id], owner_shift[slot_id])

    first_slot = lax.axis_index("facet") * SLOTS
    summed = lax.map(own_slot, first_slot + jnp.arange(SLOTS, dtype=jnp.int32))
    return (summed * scale)[None]


def solution(mesh):
    placed = (
        P(None, "facet", None, None, "col"),
        P("facet"),
        P(),
        P(),
        P("col", None),
        P("col", None),
    )
    return jax.shard_map(
        per_device,
        mesh=mesh,
        in_specs=placed,
        out_specs=P("col", "facet", None, None),
        check_vma=False,
    )
```

profile of v0, /device:TPU:0, one launch (start us, length us, event | category | flops | bytes accessed | tf_op | source)
XLA Modules:
  0.0 140.9 jit_solution(5407549524900106008)
XLA Ops:
  6.5 0.0 reduce-scatter.2.cloned.1.call-start
  7.2 0.0 copy-start.3
  7.2 0.0 copy-start
  7.2 9.3 %fusion.16 = (f32[1024,512]{1,0:T(8,128)S(1)}, f32[1024,512]{1,0:T(8,128)S(1)}) fusion(s32[1024]{0:T(1024)S(1)} %get-tuple-element.42, s32[1024]{0:T(1024)S(1)} %get-tuple-element.43), kind=kLoop, calls=%fused_computation.29 | loop fusion | flops 14680064 | bytes 4202496 | tf_op jit(solution)/shard_map/cos | solution.py:68
  16.5 0.0 copy-done.3
  16.5 0.2 fusion.40
  16.8 0.0 copy-done
  16.8 0.3 fusion.62
  17.2 0.4 multiply_add_fusion
  17.6 0.4 pad_maximum_fusion
  18.0 10.6 %fusion = f32[768,1024]{1,0:T(8,128)S(1)} fusion(f32[768,1024]{1,0:T(8,128)S(1)} %bitcast.23, f32[1024,512]{1,0:T(8,128)S(1)} %get-tuple-element.39, f32[1024,512]{1,0:T(8,128)S(1)} %get-tuple-element.38), kind=kOutput, calls=%fused_computation | convolution fusion | flops 9664724992 | bytes 10485760 | tf_op jit(solution)/shard_map/dot_general | solution.py:28
  28.6 0.4 fusion.61
  29.0 0.3 slice_add_fusion.1
  29.3 0.0 copy-start.4
  29.4 0.0 copy-start.5
  29.4 0.0 copy-start.2
  29.4 1.3 pad_maximum_fusion.1
  30.7 0.0 reduce-scatter.2.cloned.1.call-update
  30.7 0.3 all-reduce.2.cloned.1.call-start
  31.0 0.0 copy-done.4
  31.0 0.0 copy-done.5
  31.0 0.6 constant_dynamic-slice_fusion
  33.5 0.6 fusion.63
  34.1 34.9 %reduce-scatter.2.cloned.1.call-done = f32[2,48,1024]{2,1,0:T(8,128)} async-done(((f32[8,48,1024]{2,1,0:T(8,128)}), f32[2,48,1024]{2,1,0:T(8,128)}) %reduce-scatter.2.cloned.1.call-update) | async-done | bytes 393232 | tf_op jit(solution)/shard_map/reduce_scatter | solution.py:69
  69.0 0.0 all-reduce.2.cloned.1.call-update
  69.0 1.2 and_select_fusion
  70.2 0.6 add_select_fusion.9
  70.9 54.4 %all-reduce.2.cloned.1.call-done = f32[2,48,1024]{2,1,0:T(8,128)} async-done(((f32[2,48,1024]{2,1,0:T(8,128)}), f32[2,48,1024]{2,1,0:T(8,128)}) %all-reduce.2.cloned.1.call-update) | async-done | bytes 393232 | tf_op jit(solution)/shard_map/psum | solution.py:84
  125.3 3.8 %fusion.25 = f32[512,1024]{1,0:T(8,128)S(1)} fusion(f32[2,48,1024]{2,1,0:T(8,128)} %all-reduce.2.cloned.1.call-done, s32[]{:T(128)S(6)} %select_n.215, s32[48]{0:T(128)S(1)} %get-tuple-element.44, s32[48]{0:T(128)S(1)} %get-tuple-element.45, s32[512]{0:T(512)S(1)} %add_select_fusion.9), kind=kOutput, calls=%fused_computation.48 | convolution fusion | flops 302678016 | bytes 2296196 | tf_op jit(solution)/shard_map/while/body/eval_jaxpr/dot_general | solution.py:46
  129.2 2.8 %fusion.23 = f32[512,1024]{1,0:T(8,128)S(1)} fusion(f32[2,48,1024]{2,1,0:T(8,128)S(1)} %copy-done.1, s32[]{:T(128)S(6)} %select_n.215, s32[48]{0:T(128)S(1)} %get-tuple-element.44, s32[48]{0:T(128)S(1)} %get-tuple-element.45, s32[512]{0:T(512)S(1)} %add_select_fusion.9), kind=kOutput, calls=%fused_computation.46 | convolution fusion | flops 302678016 | bytes 2296836 | tf_op jit(solution)/shard_map/while/body/eval_jaxpr/dot_general | solution.py:49
  132.0 0.5 fusion.14
  132.5 1.5 %maximum_multiply_fusion = f32[1,1,512,1024]{3,2,1,0:T(8,128)} fusion(f32[1,1,512,512]{3,2,1,0:T(8,128)S(1)} %get-tuple-element.18, f32[1,1,512,512]{3,2,1,0:T(8,128)S(1)} %get-tuple-element.17), kind=kLoop, calls=%fused_computation.17 | loop fusion | flops 1048576 | bytes 4194304 | tf_op jit(solution)/shard_map/mul | solution.py:91
  (6 shorter events, 0.1 us)
Async XLA Ops:
  6.5 62.5 %reduce-scatter.2.cloned.1.call-start = ((), (), s32[]{:S(2)}) async-start(), calls=%async_computation.1 | async-start | bytes 1966080 | tf_op jit(solution)/shard_map/reduce_scatter | solution.py:69
  7.2 9.3 %copy-start.3 = (s32[8]{0:T(128)S(1)}, s32[8]{0:T(128)}, u32[]{:S(2)}) copy-start(s32[8]{0:T(128)} %param.9) | copy-start | bytes 100
  7.2 9.6 %copy-start = (f32[2,1,24,2,1024]{4,3,2,1,0:T(2,128)S(1)}, f32[2,1,24,2,1024]{4,3,2,1,0:T(2,128)}, u32[]{:S(2)}) copy-start(f32[2,1,24,2,1024]{4,3,2,1,0:T(2,128)} %param.6) | copy-start | bytes 1179652
  29.3 1.6 %copy-start.4 = (s32[1,8]{1,0:T(1,128)S(1)}, s32[1,8]{1,0:T(1,128)}, u32[]{:S(2)}) copy-start(s32[1,8]{1,0:T(1,128)} %param.10) | copy-start | bytes 100
  29.4 1.6 %copy-start.5 = (s32[1,8]{1,0:T(1,128)S(1)}, s32[1,8]{1,0:T(1,128)}, u32[]{:S(2)}) copy-start(s32[1,8]{1,0:T(1,128)} %param.11) | copy-start | bytes 100
  29.4 4.1 %copy-start.2 = (s32[2]{0:T(128)S(1)}, s32[2]{0:T(128)}, u32[]{:S(2)}) copy-start(s32[2]{0:T(128)} %param.8) | copy-start | bytes 28
  30.7 94.6 %all-reduce.2.cloned.1.call-start = ((), (), s32[]{:S(2)}) async-start(), calls=%async_computation.2 | async-start | bytes 786432 | tf_op jit(solution)/shard_map/psum | solution.py:84
  125.3 3.8 %copy-start.1 = (f32[2,48,1024]{2,1,0:T(8,128)S(1)}, f32[2,48,1024]{2,1,0:T(8,128)}, u32[]{:S(2)}) copy-start(f32[2,48,1024]{2,1,0:T(8,128)} %all-reduce.2.cloned.1.call-done) | copy-start | bytes 1179652
Sparse Core Ops, SparseCore 0:
  30.8 38.1 reduce-scatter.1
  72.1 53.2 all-reduce.1
where the time goes:
time: 141 us
  waiting for transfers between devices  89.4 us (63%)
  matrix products  17.2 us (12%)
  between operations  16.2 us (11%)
  other arithmetic  15.9 us (11%)
  local copies, waits for them, and re-layouts  1.98 us (1%)
    psum x1, waiting for transfers between devices, per_device(): merged = lax.psum(owned, 'facet')  54.4 us
    reduce_scatter x1, waiting for transfers between devices, per_device(): lax.psum_scatter(column_part(real_part, imag_part, shifted, table, col_u,...  34.9 us
    dot_general x1, matrix products, column_part(): jnp.dot(stacked, table, precision=lax.Precision.HIGHEST, preferred_elemen...  10.6 us
    cos x1, other arithmetic, per_device(): jnp.cos(table_angle)  9.29 us
    dot_general x1, matrix products, slot_term(): jnp.dot(cosine, chosen, precision=lax.Precision.HIGHEST, preferred_elemen...  3.81 us
    dot_general x1, matrix products, slot_term(): jnp.dot(sine, chosen, precision=lax.Precision.HIGHEST, preferred_element_...  2.82 us
  transfers between devices with their start and end apart: 2, of which 2 were waited for; matrix products, arithmetic and copies ran while one was open for 2% of the time, Pallas kernels for 0%

commit v1 on v0

--- a/solution.py
+++ b/solution.py
@@ -81,7 +81,7 @@
     scale = 1.0 / math.sqrt(2.0 * FS * band_rows * lax.axis_size("facet"))
     owner_cols = slot_col[0]
     owner_shift = slot_v[0]
-    merged = lax.psum(owned, "facet")
+    merged = jnp.sum(lax.all_gather(owned, "facet"), axis=0)
 
     def own_slot(slot_id):
         return slot_term(merged, row_cells, img, owner_cols[slot_id], owner_shift[slot_id])

time: 141 us -> 119 us (0.84)
  waiting for transfers between devices: 89.4 us -> 65.8 us
  other arithmetic: 15.9 us -> 18.1 us
    psum x1 -> x0, waiting for transfers between devices: 54.4 us -> none  [per_device(): merged = lax.psum(owned, 'facet')]
    all_gather x0 -> x1, waiting for transfers between devices: none -> 27.7 us  [per_device(): merged = jnp.sum(lax.all_gather(owned, 'facet'), axis=0)]
    reduce_scatter x1, waiting for transfers between devices: 34.9 us -> 38 us  [per_device(): lax.psum_scatter(column_part(real_part, imag_part, shifted, table, col_u,...]
    reduce_sum x0 -> x1, other arithmetic: none -> 2.17 us  [per_device(): merged = jnp.sum(lax.all_gather(owned, 'facet'), axis=0)]
  transfers between devices with their start and end apart: 2 -> 2, of which waited for: 2 -> 2; matrix products, arithmetic and copies ran while one was open for 2% -> 3% of each run, Pallas kernels for 0% -> 0%
where the time goes in v1:
time: 119 us
  waiting for transfers between devices  65.8 us (55%)
  other arithmetic  18.1 us (15%)
  matrix products  16.2 us (14%)
  between operations  16.2 us (14%)
  local copies, waits for them, and re-layouts  2.04 us (2%)
    reduce_scatter x1, waiting for transfers between devices, per_device(): lax.psum_scatter(column_part(real_part, imag_part, shifted, table, col_u,...  38 us
    all_gather x1, waiting for transfers between devices, per_device(): merged = jnp.sum(lax.all_gather(owned, 'facet'), axis=0)  27.7 us
    dot_general x1, matrix products, column_part(): jnp.dot(stacked, table, precision=lax.Precision.HIGHEST, preferred_elemen...  10.6 us
    cos x1, other arithmetic, per_device(): jnp.cos(table_angle)  9.29 us
    dot_general x1, matrix products, slot_term(): jnp.dot(sine, chosen, precision=lax.Precision.HIGHEST, preferred_element_...  2.82 us
    dot_general x1, matrix products, slot_term(): jnp.dot(cosine, chosen, precision=lax.Precision.HIGHEST, preferred_elemen...  2.82 us
  transfers between devices with their start and end apart: 2, of which 2 were waited for; matrix products, arithmetic and copies ran while one was open for 3% of the time, Pallas kernels for 0%

profile of v1, /device:TPU:0, one launch (start us, length us, event | category | flops | bytes accessed | tf_op | source)
XLA Modules:
  0.0 118.6 jit_solution(2886062862298222277)
XLA Ops:
  6.5 0.0 reduce-scatter.2.cloned.1.call-start
  7.2 0.0 copy-start.2
  7.2 0.0 copy-start
  7.2 9.3 %fusion.16 = (f32[1024,512]{1,0:T(8,128)S(1)}, f32[1024,512]{1,0:T(8,128)S(1)}) fusion(s32[1024]{0:T(1024)S(1)} %get-tuple-element.42, s32[1024]{0:T(1024)S(1)} %get-tuple-element.43), kind=kLoop, calls=%fused_computation.29 | loop fusion | flops 14680064 | bytes 4202496 | tf_op jit(solution)/shard_map/cos | solution.py:68
  16.5 0.0 copy-done.2
  16.5 0.2 fusion.40
  16.8 0.0 copy-done
  16.8 0.3 fusion.62
  17.2 0.4 multiply_add_fusion
  17.6 0.4 pad_maximum_fusion
  18.0 10.6 %fusion = f32[768,1024]{1,0:T(8,128)S(1)} fusion(f32[768,1024]{1,0:T(8,128)S(1)} %bitcast.24, f32[1024,512]{1,0:T(8,128)S(1)} %get-tuple-element.39, f32[1024,512]{1,0:T(8,128)S(1)} %get-tuple-element.38), kind=kOutput, calls=%fused_computation | convolution fusion | flops 9664724992 | bytes 10485760 | tf_op jit(solution)/shard_map/dot_general | solution.py:28
  28.6 0.4 fusion.61
  29.0 0.3 slice_add_fusion.1
  29.3 0.0 copy-start.3
  29.4 0.0 copy-start.4
  29.4 0.0 copy-start.1
  29.4 1.3 %pad_maximum_fusion.1 = f32[8,48,1024]{2,1,0:T(8,128)} fusion(f32[8,48,512]{2,1,0:T(8,128)S(1)} %get-tuple-element.20, f32[8,48,512]{2,1,0:T(8,128)S(1)} %get-tuple-element.19), kind=kLoop, calls=%fused_computation.21 | loop fusion | flops 393216 | bytes 3145728 | tf_op jit(solution)/shard_map/concatenate | solution.py:36
  30.7 0.0 reduce-scatter.2.cloned.1.call-update
  30.7 0.3 all-gather.3.cloned.1.call-start
  31.0 38.0 %reduce-scatter.2.cloned.1.call-done = f32[2,48,1024]{2,1,0:T(8,128)} async-done(((f32[8,48,1024]{2,1,0:T(8,128)}), f32[2,48,1024]{2,1,0:T(8,128)}) %reduce-scatter.2.cloned.1.call-update) | async-done | bytes 393232 | tf_op jit(solution)/shard_map/reduce_scatter | solution.py:69
  69.0 0.0 all-gather.3.cloned.1.call-update
  69.0 0.0 copy-done.3
  69.0 0.6 constant_dynamic-slice_fusion
  71.6 0.7 fusion.63
  72.3 1.4 %and_select_fusion = (s32[48]{0:T(128)S(1)}, s32[48]{0:T(128)S(1)}) fusion(s32[]{:T(128)} %bitcast.2, s32[]{:T(128)} %bitcast.1), kind=kLoop, calls=%fused_computation.91 | loop fusion | flops 2160 | bytes 392 | tf_op jit(solution)/shard_map/while/body/eval_jaxpr/jit(remainder)/select_n | solution.py:15
  73.6 0.6 add_select_fusion.9
  74.2 27.7 %all-gather.3.cloned.1.call-done = f32[16,48,1024]{2,1,0:T(8,128)} async-done(((f32[2,48,1024]{2,1,0:T(8,128)}), f32[16,48,1024]{2,1,0:T(8,128)}) %all-gather.3.cloned.1.call-update) | async-done | bytes 3145744 | tf_op jit(solution)/shard_map/all_gather | solution.py:84
  101.9 2.2 %reduce_sum.9 = f32[2,48,1024]{2,1,0:T(8,128)S(1)} reduce(f32[8,2,48,1024]{3,2,1,0:T(8,128)} %bitcast.25, f32[]{:T(128)} %constant.192.clone.1), dimensions={0}, to_apply=%region_1.2 | reduce | flops 688128 | bytes 3538948 | tf_op jit(solution)/shard_map/reduce_sum | solution.py:84
  104.1 2.8 %fusion.25 = f32[512,1024]{1,0:T(8,128)S(1)} fusion(f32[2,48,1024]{2,1,0:T(8,128)S(1)} %reduce_sum.9, s32[]{:T(128)S(6)} %select_n.215, s32[48]{0:T(128)S(1)} %get-tuple-element.44, s32[48]{0:T(128)S(1)} %get-tuple-element.45, s32[512]{0:T(512)S(1)} %add_select_fusion.9), kind=kOutput, calls=%fused_computation.48 | convolution fusion | flops 302678016 | bytes 2296836 | tf_op jit(solution)/shard_map/while/body/eval_jaxpr/dot_general | solution.py:46
  106.9 2.8 %fusion.23 = f32[512,1024]{1,0:T(8,128)S(1)} fusion(f32[2,48,1024]{2,1,0:T(8,128)S(1)} %reduce_sum.9, s32[]{:T(128)S(6)} %select_n.215, s32[48]{0:T(128)S(1)} %get-tuple-element.44, s32[48]{0:T(128)S(1)} %get-tuple-element.45, s32[512]{0:T(512)S(1)} %add_select_fusion.9), kind=kOutput, calls=%fused_computation.46 | convolution fusion | flops 302678016 | bytes 2296836 | tf_op jit(solution)/shard_map/while/body/eval_jaxpr/dot_general | solution.py:49
  109.8 0.5 fusion.14
  110.3 1.5 %maximum_multiply_fusion = f32[1,1,512,1024]{3,2,1,0:T(8,128)} fusion(f32[1,1,512,512]{3,2,1,0:T(8,128)S(1)} %get-tuple-element.18, f32[1,1,512,512]{3,2,1,0:T(8,128)S(1)} %get-tuple-element.17), kind=kLoop, calls=%fused_computation.17 | loop fusion | flops 1048576 | bytes 4194304 | tf_op jit(solution)/shard_map/mul | solution.py:91
  (5 shorter events, 0.1 us)
Async XLA Ops:
  6.5 62.5 %reduce-scatter.2.cloned.1.call-start = ((), (), s32[]{:S(2)}) async-start(), calls=%async_computation.1 | async-start | bytes 1966080 | tf_op jit(solution)/shard_map/reduce_scatter | solution.py:69
  7.2 9.3 %copy-start.2 = (s32[8]{0:T(128)S(1)}, s32[8]{0:T(128)}, u32[]{:S(2)}) copy-start(s32[8]{0:T(128)} %param.9) | copy-start | bytes 100
  7.2 9.6 %copy-start = (f32[2,1,24,2,1024]{4,3,2,1,0:T(2,128)S(1)}, f32[2,1,24,2,1024]{4,3,2,1,0:T(2,128)}, u32[]{:S(2)}) copy-start(f32[2,1,24,2,1024]{4,3,2,1,0:T(2,128)} %param.6) | copy-start | bytes 1179652
  29.3 39.7 %copy-start.3 = (s32[1,8]{1,0:T(1,128)S(1)}, s32[1,8]{1,0:T(1,128)}, u32[]{:S(2)}) copy-start(s32[1,8]{1,0:T(1,128)} %param.10) | copy-start | bytes 100
  29.4 39.7 %copy-start.4 = (s32[1,8]{1,0:T(1,128)S(1)}, s32[1,8]{1,0:T(1,128)}, u32[]{:S(2)}) copy-start(s32[1,8]{1,0:T(1,128)} %param.11) | copy-start | bytes 100
  29.4 42.2 %copy-start.1 = (s32[2]{0:T(128)S(1)}, s32[2]{0:T(128)}, u32[]{:S(2)}) copy-start(s32[2]{0:T(128)} %param.8) | copy-start | bytes 28
  30.7 71.3 %all-gather.3.cloned.1.call-start = ((), (), s32[]{:S(2)}) async-start(), calls=%async_computation.2 | async-start | bytes 3538944 | tf_op jit(solution)/shard_map/all_gather | solution.py:84
Sparse Core Ops, SparseCore 0:
  30.8 38.1 reduce-scatter.1
  70.9 31.0 all-gather.2
